TPU v7x, 32 devices: a whole 2x2x4 slice. The times are simulated.
32 devices in a mesh: group: 2 (over y), ctx: 4 (over z), head: 4 (over x, core).
Axes of the slice: x: 2, y: 2, z: 4, core: 2. Of those that a mesh axis runs over, the one named last changes fastest.
Arguments:
- mixer_x: bfloat16 [2048, 8192], P(('group', 'ctx'), 'head'), parts along dimension 0, may hold values from -6 to 6
- mixer_bc: bfloat16 [2, 2048, 1024], P(None, ('group', 'ctx'), 'head'), parts along dimension 1, may hold values from -3 to 3
- mixer_gate: bfloat16 [2048, 8192], P(('group', 'ctx'), 'head'), parts along dimension 0, may hold values from -9 to 9
- step_logits: float32 [2048, 128], P(('group', 'ctx'), 'head'), parts along dimension 0, may hold values from -3 to 3
- conv_x_weight: float32 [4, 8192], P(None, 'head'), may hold values from -0.6 to 0.6
- conv_bc_weight: float32 [2, 4, 1024], P(None, None, 'head'), may hold values from -0.6 to 0.6
- head_params: float32 [3, 128], P(None, 'head'), as said below
- norm_gain: float32 [8192], P('head'), may hold values from 0.5 to 1.5
- grad_output: bfloat16 [2048, 8192], P(('group', 'ctx'), 'head'), parts along dimension 0, may hold values from -9 to 9
Outputs:
- grad_x: bfloat16 [2048, 8192], P(('group', 'ctx'), 'head'), parts along dimension 0
- grad_bc: bfloat16 [2, 2048, 1024], P(None, ('group', 'ctx'), 'head'), parts along dimension 1
- grad_gate: bfloat16 [2048, 8192], P(('group', 'ctx'), 'head'), parts along dimension 0
- grad_step: float32 [2048, 128], P(('group', 'ctx'), 'head'), parts along dimension 0
- grad_conv_x: float32 [8, 8192], P('group', 'head'), parts along dimension 0
- grad_conv_bc: float32 [4, 4, 1024], P('group', None, 'head'), parts along dimension 0
- grad_heads: float32 [6, 128], P('group', 'head'), parts along dimension 0
- grad_gain: float32 [16384], P(('group', 'head')), parts along dimension 0
There are 2 independent parts, one for each index of `group`. A program takes and returns all parts, laid end to end along the dimension named above; an argument that names none is the same for every part. Nothing has to cross between parts.
Inputs may be any that keep to these rules, and one draw needn't show every extreme that they name: `head_params`: row 0 is added to the step logits and lies between -1 and 1; row 1 is the logarithm of a decay rate between log(0.2 / 1024) and log(0.1); row 2 is a skip factor between 0.5 and 1.5.
All inputs are finite; a program needn't handle non-finite values.
Results may differ from a plain program's by a relative error of at most 0.014.
Values may be sent and summed in bfloat16 or wider, within the bound.
A program may use at most 128 MiB of HBM per device.

v0:
```python
import jax
import jax.numpy as jnp
from jax import lax
from jax.sharding import PartitionSpec as P

HEADS = 128
HEAD_DIM = 64
STATE = 128
GROUPS = 8
CONV = 4
SPAN = 256
INNER = 8192
epsilon = 1e-05


def passed_along(shard, axis, by):
    size = lax.axis_size(axis)
    pairs = [(i, i + by) for i in range(size) if 0 <= i + by < size]
    return lax.ppermute(shard, axis, pairs)


def entering_2(shard, axis, combine, identity):
    size, position = (lax.axis_size(axis), lax.axis_index(axis))
    everything = jax.tree.map(
        lambda part, kind: lax.all_gather(part.astype(kind), axis),
        shard,
        (jnp.bfloat16, jnp.bfloat16),
    )
    start = jax.tree.map(
        lambda part, zero: jnp.broadcast_to(jnp.asarray(zero, part.dtype), part.shape),
        shard,
        identity,
    )

    def entering_step(k, before):
        reached = k < position
        new = combine(
            before, jax.tree.map(lambda part, own: part[k].astype(own.dtype), everything, shard)
        )
        return jax.tree.map(lambda a, b: jnp.where(reached, a, b), new, before)

    return lax.fori_loop(0, size, entering_step, start)


def prefix(shard, axis, combine, identity):
    size, position = (lax.axis_size(axis), lax.axis_index(axis))
    everything = jax.tree.map(
        lambda part, kind: lax.all_gather(part.astype(kind), axis),
        shard,
        jax.tree.map(lambda a: jnp.bfloat16 if a.dtype == jnp.float32 else a.dtype, shard),
    )
    start = jax.tree.map(
        lambda part, zero: jnp.broadcast_to(jnp.asarray(zero, part.dtype), part.shape),
        shard,
        identity,
    )

    def prefix_step(k, before):
        at = size - 1 - k
        reached = at > position
        new = combine(
            before, jax.tree.map(lambda part, own: part[at].astype(own.dtype), everything, shard)
        )
        return jax.tree.map(lambda a, b: jnp.where(reached, a, b), new, before)

    return lax.fori_loop(0, size, prefix_step, start)


def conv_silu(padded_rows, kernel):
    taps_count = kernel.shape[0]
    out_rows = padded_rows.shape[0] - taps_count + 1
    summed = kernel[0] * padded_rows[0:out_rows]
    for offset in range(1, taps_count):
        summed = summed + kernel[offset] * padded_rows[offset : offset + out_rows]
    return jax.nn.silu(summed).astype(jnp.bfloat16)


def span_parts(x_block, b_block, c_block, step_block, decay_rate, skip_gain):
    log_decay = jnp.cumsum(step_block * decay_rate, axis=0)
    block_end = log_decay[-1]
    scores = jnp.einsum("tgn,sgn->gts", c_block, b_block, preferred_element_type=jnp.float32)
    by_head = jnp.transpose(log_decay, (1, 2, 0))
    spread = by_head[:, :, :, None] - by_head[:, :, None, :]
    positions = jnp.arange(log_decay.shape[0])
    causal = positions[:, None] >= positions[None, :]
    weights = jnp.where(causal, jnp.exp(jnp.where(causal, spread, 0.0)), 0.0)
    step_heads = jnp.transpose(step_block, (1, 2, 0))
    mixing = (scores[:, None] * weights * step_heads[:, :, None, :]).astype(jnp.bfloat16)
    inside = jnp.einsum("gkts,sgkp->tgkp", mixing, x_block, preferred_element_type=jnp.float32)
    inside = inside + skip_gain[None, :, :, None] * x_block.astype(jnp.float32)
    carry_weight = jnp.exp(block_end[None] - log_decay) * step_block
    scaled_x = (x_block.astype(jnp.float32) * carry_weight[..., None]).astype(jnp.bfloat16)
    block_state = jnp.einsum(
        "sgkp,sgn->gkpn", scaled_x, b_block, preferred_element_type=jnp.float32
    )
    return (inside, block_state, block_end, log_decay)


def state_read(c_block, state_low, log_decay):
    readout = jnp.einsum("tgn,gkpn->tgkp", c_block, state_low, preferred_element_type=jnp.float32)
    return readout * jnp.exp(log_decay)[..., None]


def join_states(earlier, later):
    return (earlier[0] + later[0], jnp.exp(later[0])[..., None, None] * earlier[1] + later[1])


def shards(
    mixer_x,
    mixer_bc,
    mixer_gate,
    step_logits,
    conv_x_weight,
    conv_bc_weight,
    head_params,
    norm_gain,
    grad_output,
):
    margin = CONV - 1
    length_dev = mixer_x.shape[0]
    width_dev = mixer_x.shape[1]
    columns = mixer_bc.shape[2]
    groups = columns // STATE
    per_group = HEADS // GROUPS
    blocks = length_dev // SPAN
    rim_rows = jnp.concatenate(
        [
            mixer_x[length_dev - margin :],
            mixer_bc[0, length_dev - margin :],
            mixer_bc[1, length_dev - margin :],
        ],
        axis=1,
    )
    before = passed_along(rim_rows, "ctx", 1)

    def prepare(x_own, bc_own, borrowed, step_own, conv_x, conv_bc, params_own):
        x_rows = jnp.concatenate([borrowed[:, :width_dev], x_own], axis=0)
        b_rows = jnp.concatenate([borrowed[:, width_dev : width_dev + columns], bc_own[0]], axis=0)
        c_rows = jnp.concatenate([borrowed[:, width_dev + columns :], bc_own[1]], axis=0)
        x_conv = conv_silu(x_rows, conv_x)
        b_conv = conv_silu(b_rows, conv_bc[0])
        c_conv = conv_silu(c_rows, conv_bc[1])
        step_size = jax.nn.softplus(step_own + params_own[0])
        decay_rate = (-jnp.exp(params_own[1])).reshape(groups, per_group)
        skip_gain = params_own[2].reshape(groups, per_group)
        x_blocks = x_conv.reshape(blocks, SPAN, groups, per_group, HEAD_DIM)
        b_blocks = b_conv.reshape(blocks, SPAN, groups, STATE)
        c_blocks = c_conv.reshape(blocks, SPAN, groups, STATE)
        step_blocks = step_size.reshape(blocks, SPAN, groups, per_group)
        inside_all, block_states, block_ends, log_decays = jax.vmap(
            span_parts, in_axes=(0, 0, 0, 0, None, None)
        )(x_blocks, b_blocks, c_blocks, step_blocks, decay_rate, skip_gain)
        return (inside_all, block_states, block_ends, log_decays, c_blocks)

    primals = (
        mixer_x.astype(jnp.float32),
        mixer_bc.astype(jnp.float32),
        before.astype(jnp.float32),
        step_logits,
        conv_x_weight,
        conv_bc_weight,
        head_params,
    )
    prepared, pull_prepare = jax.vjp(prepare, *primals)
    inside_all, block_states, block_ends, log_decays, c_blocks = prepared
    device_log = block_ends[0]
    device_state = block_states[0]
    empty_log = jnp.zeros_like(device_log)
    empty_state = jnp.zeros_like(device_state)
    halfway = per_group // 2
    lower_half = entering_2(
        (device_log[:, :halfway], device_state[:, :halfway]),
        "ctx",
        join_states,
        (empty_log[:, :halfway], empty_state[:, :halfway]),
    )
    upper_half = entering_2(
        (device_log[:, halfway:], device_state[:, halfway:]),
        "ctx",
        join_states,
        (empty_log[:, halfway:], empty_state[:, halfway:]),
    )
    carried = jnp.concatenate([lower_half[1], upper_half[1]], axis=1)
    number = 0
    entering = [carried]
    entering_low = jnp.stack(entering).astype(jnp.bfloat16)

    def read_all(c_part, state_part, decay_part):
        return jax.vmap(state_read)(c_part, state_part, decay_part)

    readouts, pull_read = jax.vjp(read_all, c_blocks, entering_low, log_decays)
    mixed = (inside_all + readouts).reshape(length_dev, width_dev)
    gate_value = mixer_gate.astype(jnp.float32)
    sigmoid_z = jax.nn.sigmoid(gate_value)
    gate_act = gate_value * sigmoid_z
    gated = mixed * gate_act
    upstream = grad_output.astype(jnp.float32) * norm_gain
    own_square = jnp.sum(gated * gated, axis=1)
    square = lax.psum(own_square, "head")
    factor = lax.rsqrt(square / INNER + epsilon)
    normed = gated * factor[:, None]
    projected = lax.psum(jnp.sum(upstream * normed, axis=1), "head")
    d_gated = (upstream - normed * (projected / INNER)[:, None]) * factor[:, None]
    grad_gain_own = jnp.sum(grad_output.astype(jnp.float32) * normed, axis=0)
    d_mixed = d_gated * gate_act
    grad_gate = (d_gated * mixed * (sigmoid_z * (1.0 + gate_value * (1.0 - sigmoid_z)))).astype(
        jnp.bfloat16
    )
    grad_blocks = d_mixed.reshape(inside_all.shape)
    d_c_read, d_entering_low, d_decay_read = pull_read(grad_blocks)
    d_entering = d_entering_low.astype(jnp.float32)
    pending = jnp.zeros_like(carried)
    after_zero = [None] * blocks
    for number in reversed(range(blocks)):
        after_zero[number] = pending
        pending = d_entering[number] + jnp.exp(block_ends[number])[..., None, None] * pending
    outgoing = prefix((device_log, pending), "ctx", join_states, (empty_log, empty_state))[1]
    decay_after = jnp.zeros_like(device_log)
    grad_states = [None] * blocks
    grad_ends = [None] * blocks
    for number in reversed(range(blocks)):
        state_grad = after_zero[number] + jnp.exp(decay_after)[..., None, None] * outgoing
        grad_states[number] = state_grad
        grad_ends[number] = jnp.exp(block_ends[number]) * jnp.sum(
            state_grad * entering[number], axis=(2, 3)
        )
        decay_after = block_ends[number]
    gradients = pull_prepare(
        (grad_blocks, jnp.stack(grad_states), jnp.stack(grad_ends), d_decay_read, d_c_read)
    )
    returned = passed_along(gradients[2], "ctx", -1)
    grad_x = (
        gradients[0].at[length_dev - margin :].add(returned[:, :width_dev]).astype(jnp.bfloat16)
    )
    grad_b = (
        gradients[1][0].at[length_dev - margin :].add(returned[:, width_dev : width_dev + columns])
    )
    grad_c = gradients[1][1].at[length_dev - margin :].add(returned[:, width_dev + columns :])
    grad_bc = jnp.stack([grad_b, grad_c]).astype(jnp.bfloat16)
    totals = lax.psum((gradients[4], gradients[5], gradients[6], grad_gain_own), "ctx")
    return (grad_x, grad_bc, grad_gate, gradients[3], totals[0], totals[1], totals[2], totals[3])


def solution(mesh):
    return jax.shard_map(
        shards,
        mesh=mesh,
        in_specs=(
            P(("group", "ctx"), "head"),
            P(None, ("group", "ctx"), "head"),
            P(("group", "ctx"), "head"),
            P(("group", "ctx"), "head"),
            P(None, "head"),
            P(None, None, "head"),
            P(None, "head"),
            P("head"),
            P(("group", "ctx"), "head"),
        ),
        out_specs=(
            P(("group", "ctx"), "head"),
            P(None, ("group", "ctx"), "head"),
            P(("group", "ctx"), "head"),
            P(("group", "ctx"), "head"),
            P("group", "head"),
            P("group", None, "head"),
            P("group", "head"),
            P(("group", "head")),
        ),
        check_vma=False,
    )
```

profile of v0, /device:TPU:0, one launch (start us, length us, event | category | flops | bytes accessed | tf_op | source)
XLA Modules:
  0.0 249.9 jit_solution(2895747203639951558)
XLA Ops:
  8.7 5.0 %collective-permute-start = (bf16[3,2560]{1,0:T(4,128)(2,1)S(1)}, bf16[3,2560]{1,0:T(4,128)(2,1)S(1)}, u32[]{:S(2)}, u32[]{:S(2)}) collective-permute-start(bf16[3,2560]{1,0:T(4,128)(2,1)S(1)} %pad_maximum_fusion.4), channel_id=1, source_target_pairs={{0,4},{4,8},{8,12},{1,5},{5,9},{9,13},{2,6},{6,10},{10,14},{3,7},{... | collective-permute-start | bytes 46088 | tf_op jit(solution)/shard_map/ppermute | solution.py:19
  13.7 1.1 copy.223
  14.8 1.3 slice_reduce_fusion
  17.7 1.2 reduce-window.14
  25.7 1.3 copy.222
  27.2 6.4 %multiply_convert_fusion.5 = (bf16[256,2048]{0,1:T(8,128)(2,1)S(1)}, f32[256,2048]{0,1:T(8,128)}) fusion(f32[256,2048]{0,1:T(8,128)S(1)} %convert_element_type.286, f32[2048]{0:T(1024)S(1)} %bitcast.392, f32[3,2048]{0,1:T(8,128)} %copy.222, f32[2048]{0:T(1024)S(1)} %bitcast.394, f32[2048]{0:T(1024)S(1)} %bitcast.396, f32[2048]{0:T(1024)S(1)} %bitcast.390), kind=kLoop, calls=%fused_computation.81 | loop fusion | flops 7864320 | bytes 5300224 | tf_op jit(solution)/shard_map/jvp()/convert_element_type | solution.py:75
  33.7 1.7 multiply_convert_fusion.16
  37.4 9.1 %all-gather.7 = bf16[4,2,8]{2,1,0:T(2,128)(2,1)S(1)} all-gather(bf16[1,2,8]{2,1,0:T(2,128)(2,1)S(1)} %get-tuple-element.588), channel_id=5, replica_groups=mesh['group'=2,'ctx'=4,'head'=4] {'ctx'}, dimensions={0}, use_global_device_ids=true | all-gather | bytes 160 | tf_op jit(solution)/shard_map/all_gather | solution.py:25
  46.5 8.5 %all-gather.6 = bf16[4,2,8]{2,1,0:T(2,128)(2,1)S(1)} all-gather(bf16[1,2,8]{2,1,0:T(2,128)(2,1)S(1)} %get-tuple-element.589), channel_id=3, replica_groups=mesh['group'=2,'ctx'=4,'head'=4] {'ctx'}, dimensions={0}, use_global_device_ids=true | all-gather | bytes 160 | tf_op jit(solution)/shard_map/all_gather | solution.py:25
  57.1 2.3 copy.235
  59.4 2.3 copy.220
  62.9 1.1 fusion.124
  64.0 1.1 all-gather.14.cloned.1.call-done
  65.1 4.5 %while.48 = (s32[]{:T(128)}, f32[2,8,64,128]{3,2,1,0:T(8,128)S(1)}, s32[]{:T(128)}, bf16[4,2,8]{2,1,0:T(2,128)(2,1)S(1)}, bf16[4,2,8,64,128]{4,3,2,1,0:T(8,128)(2,1)}, /*index=5*/s32[]{:T(128)}, s32[]{:T(128)}) while((s32[]{:T(128)}, f32[2,8,64,128]{3,2,1,0:T(8,128)S(1)}, s32[]{:T(128)}, bf16[4,2,8]{2,1,0:T(2,128)(2,1)S(1)}, ...), condition=%wide.region_5.6_spmd.clone, body=%wide.region_4.5_spmd.clone.sunk | while | flops 655380 | bytes 1310985 | solution.py:42
  65.1 1.1 fusion.145
  66.2 1.1 fusion.145
  67.4 1.1 fusion.145
  68.5 1.1 fusion.145
  69.6 24.5 %all-gather.12.cloned.1.call-done = bf16[8,8,64,128]{3,2,1,0:T(8,128)(2,1)} async-done(((bf16[2,8,64,128]{3,2,1,0:T(8,128)(2,1)}), bf16[8,8,64,128]{3,2,1,0:T(8,128)(2,1)}) %all-gather.12.cloned.1.call-update) | async-done | bytes 1048592 | tf_op jit(solution)/shard_map/all_gather | solution.py:25
  94.1 4.5 %while.47 = (s32[]{:T(128)}, f32[2,8,64,128]{3,2,1,0:T(8,128)S(1)}, s32[]{:T(128)}, bf16[4,2,8]{2,1,0:T(2,128)(2,1)S(1)}, bf16[4,2,8,64,128]{4,3,2,1,0:T(8,128)(2,1)}, /*index=5*/s32[]{:T(128)}, s32[]{:T(128)}) while((s32[]{:T(128)}, f32[2,8,64,128]{3,2,1,0:T(8,128)S(1)}, s32[]{:T(128)}, bf16[4,2,8]{2,1,0:T(2,128)(2,1)S(1)}, ...), condition=%wide.region_3.4_spmd.clone, body=%wide.region_2.3_spmd.clone.sunk | while | flops 655380 | bytes 1310985 | solution.py:42
  94.1 1.1 fusion.144
  95.2 1.1 fusion.144
  96.4 1.1 fusion.144
  97.5 1.1 fusion.144
  99.9 2.8 %fusion.32 = f32[1,256,2,16,64]{1,4,3,2,0:T(8,128)S(1)} fusion(f32[2,16,64,256]{3,2,1,0:T(8,128)S(1)} %fusion.95, bf16[256,2,16,64]{0,3,2,1:T(8,128)(2,1)S(1)} %bitcast.359, f32[2,16,256]{2,1,0:T(8,128)S(1)} %bitcast.386, f32[2,16,256]{2,1,0:T(8,128)S(1)} %copy-done.61, f32[2,256,256]{2,1,0:T(8,128)S(1)} %copy-done.42, pred[256,256]{1,0:T(8,128)(4,1)S(1)} %copy-done.58, ...), kind=kOutput, calls=%fused_computation.58 | convolution fusion | flops 283639808 | bytes 6979712 | tf_op jit(solution)/shard_map/jvp(vmap(gkts,sgkp->tgkp))/dot_general | solution.py:89
  102.7 1.3 multiply_reduce_fusion.5
  104.0 6.7 %psum.42 = f32[256]{0:T(256)} all-reduce(f32[256]{0:T(256)} %multiply_reduce_fusion.5), channel_id=1, replica_groups=mesh['group'=2,'ctx'=4,'head'=4] {'head'}, use_global_device_ids=true, to_apply=%region_7.8 | all-reduce | flops 256 | bytes 2048 | tf_op jit(solution)/shard_map/psum | solution.py:199
  111.4 3.6 %fusion.20 = (f32[2048]{0:T(1024)}, f32[256]{0:T(256)}) fusion(bf16[256,2048]{0,1:T(8,128)(2,1)} %copy.220, f32[256]{0:T(256)S(1)} %add_rsqrt_fusion, bf16[256,2048]{0,1:T(8,128)(2,1)} %copy.235, f32[1,256,2,16,64]{1,4,3,2,0:T(8,128)S(1)} %fusion.32, f32[2048]{0:T(1024)} %param.28), kind=kLoop, calls=%fused_computation.44 | loop fusion | flops 6813440 | bytes 4212736 | tf_op jit(solution)/shard_map/reduce_sum | solution.py:204
  115.0 6.3 %psum.43 = f32[256]{0:T(256)S(1)} all-reduce(f32[256]{0:T(256)} %get-tuple-element.477), channel_id=1, replica_groups=mesh['group'=2,'ctx'=4,'head'=4] {'head'}, use_global_device_ids=true, to_apply=%region_9.10 | all-reduce | flops 256 | bytes 2048 | tf_op jit(solution)/shard_map/psum | solution.py:202
  121.3 4.9 %multiply_reduce_fusion = (f32[2048]{0:T(1024)}, f32[256,2048]{0,1:T(8,128)S(1)}, bf16[256,2048]{0,1:T(8,128)(2,1)}) fusion(bf16[256,2048]{0,1:T(8,128)(2,1)S(1)} %get-tuple-element.538, f32[256]{0:T(256)S(1)} %broadcast_multiply_fusion.13, f32[256]{0:T(256)} %copy-done.82, bf16[256,2048]{0,1:T(8,128)(2,1)} %copy.235, f32[1,256,2,16,64]{1,4,3,2,0:T(8,128)} %copy-done, ...), kind=kLoop, calls=%fused_computation.73 | loop fusion | flops 12056576 | bytes 8407040 | tf_op jit(solution)/shard_map/transpose(jvp(vmap()))/reduce_sum | solution.py:90
  126.2 1.2 fusion.56
  127.4 9.9 %all-gather = bf16[4,1,2,16]{3,2,1,0:T(2,128)(2,1)} all-gather(bf16[1,1,2,16]{3,2,1,0:T(2,128)(2,1)} %get-tuple-element.567), channel_id=2, replica_groups=mesh['group'=2,'ctx'=4,'head'=4] {'ctx'}, dimensions={0}, use_global_device_ids=true | all-gather | bytes 320 | tf_op jit(solution)/shard_map/all_gather | solution.py:48
  137.4 2.6 %fusion.33 = f32[256,2,16]{0,2,1:T(8,128)} fusion(f32[1,256,2,16,64]{1,4,3,2,0:T(8,128)S(1)} %bitcast.353, f32[2,16,64,256]{3,2,1,0:T(8,128)} %copy-done.14), kind=kLoop, calls=%fused_computation.61 | loop fusion | flops 1040384 | bytes 4227072 | tf_op jit(solution)/shard_map/transpose(jvp(vmap()))/reduce_sum | solution.py:101
  140.0 1.6 copy.245
  141.6 8.2 %fusion.13 = (f32[2,16,256]{2,1,0:T(8,128)}, f32[2,16,256]{2,1,0:T(8,128)}, f32[2,16,256]{2,1,0:T(8,128)}, bf16[2,256,256]{2,1,0:T(8,128)(2,1)}) fusion(f32[2,16,256]{2,1,0:T(8,128)} %bitcast.385, f32[2,16,256]{2,1,0:T(8,128)} %copy.228, f32[2,256,256]{2,1,0:T(8,128)} %fusion.124, pred[256,256]{1,0:T(8,128)(4,1)} %iota_compare_fusion, ...), kind=kOutput, calls=%fused_computation.23 | convolution fusion | flops 301834240 | bytes 4161536 | tf_op jit(solution)/shard_map/transpose(jvp(vmap(gkts,sgkp->tgkp)))/dot_general | solution.py:89
  149.8 1.6 copy.247
  151.4 1.6 copy.248
  153.0 1.6 copy.244
  154.6 1.4 reduce_sum.289
  155.9 1.4 reduce_sum.293
  157.3 1.3 reshape.693
  158.7 2.3 copy.258
  160.9 1.9 fusion.70
  162.8 1.6 fusion.63
  165.4 6.9 %all-gather.16.cloned.1.call-done = bf16[8,16,64,128]{3,2,1,0:T(8,128)(2,1)} async-done(((bf16[2,16,64,128]{3,2,1,0:T(8,128)(2,1)}), bf16[8,16,64,128]{3,2,1,0:T(8,128)(2,1)}) %all-gather.16.cloned.1.call-update) | async-done | bytes 2097168 | tf_op jit(solution)/shard_map/all_gather | solution.py:48
  172.2 7.9 %while.49 = (s32[]{:T(128)}, f32[2,16,64,128]{3,2,1,0:T(8,128)S(1)}, s32[]{:T(128)}, bf16[4,2,16]{2,1,0:T(2,128)(2,1)}, bf16[4,2,16,64,128]{4,3,2,1,0:T(8,128)(2...) while((s32[]{:T(128)}, f32[2,16,64,128]{3,2,1,0:T(8,128)S(1)}, s32[]{:T(128)}, ...), condition=%wide.region_11.12_spmd.clone, body=%wide.region_10.11_spmd.clone.sunk | while | flops 1310760 | bytes 2621927 | solution.py:66
  172.9 1.3 fusion.146
  174.9 1.3 fusion.146
  176.9 1.3 fusion.146
  178.9 1.3 fusion.146
  180.2 2.1 multiply_reduce_fusion.6
  182.4 1.1 fusion.37
  184.0 1.7 multiply_reduce_fusion.14
  189.2 3.3 %fusion.59 = bf16[1,256,2,16,64]{1,4,3,2,0:T(8,128)(2,1)S(1)} fusion(f32[2,16,64,256]{3,2,1,0:T(8,128)S(1)} %bitcast.356, f32[2,16,256]{2,1,0:T(8,128)S(1)} %bitcast.387, f32[2,16,256]{2,1,0:T(8,128)S(1)} %copy-done.62, f32[2,256,256]{2,1,0:T(8,128)S(1)} %copy-done.43, pred[256,256]{1,0:T(8,128)(4,1)S(1)} %copy-done.59, ...), kind=kOutput, calls=%fused_computation.96 | convolution fusion | flops 284688384 | bytes 6979712 | tf_op jit(solution)/shard_map/transpose(jvp(vmap(gkts,sgkp->tgkp)))/dot_general | solution.py:89
  192.5 4.1 %multiply_reduce_fusion.3 = (f32[2048]{0:T(1024)S(1)}, f32[2048]{0:T(1024)S(1)}, f32[2048]{0:T(1024)S(1)}, f32[2048]{0:T(1024)S(1)}, f32[256,2048]{0,1:T(8,128)S(1)}) fusion(f32[256,2048]{0,1:T(8,128)S(1)} %copy-done.2, f32[3,2048]{0,1:T(8,128)S(1)} %copy-done.10, bf16[256,2048]{0,1:T(8,128)(2,1)S(1)} %copy-done.9, f32[256,2048]{0,1:T(8,128)S(1)} %copy-done.13, ...), kind=kLoop, calls=%fused_computation.76 | loop fusion | flops 11526144 | bytes 8445952 | tf_op jit(solution)/shard_map/transpose(jvp())/reduce_sum | solution.py:74
  196.7 1.8 broadcast_multiply_fusion.3
  198.5 2.5 pad_add_fusion
  201.1 1.3 split.24
  204.1 5.0 %reduce-window.16 = f32[1,16,2,2,128]{4,1,2,3,0:T(8,128)S(1)} reduce-window(f32[1,16,2,2,128]{4,1,2,3,0:T(8,128)S(1)} %copy.249, f32[]{:T(128)} %constant.188.clone.1), window={size=1x1x1x1x128 pad=0_0x0_0x0_0x0_0x0_127}, to_apply=%region_20.21 | reduce-window | flops 1040384 | bytes 65540 | tf_op jit(solution)/shard_map/reduce-window.2
  212.2 1.3 collective-permute-start.1
  213.8 20.3 %all-reduce.35 = (f32[4,2048]{1,0:T(4,128)}, f32[2,4,256]{2,1,0:T(4,128)}, f32[3,32]{1,0:T(4,128)}, f32[2048]{0:T(1024)}) all-reduce(f32[4,2048]{1,0:T(4,128)S(1)} %pad_add_fusion.11, f32[2,4,256]{2,1,0:T(4,128)S(1)} %pad_add_fusion.12, f32[3,32]{1,0:T(4,128)S(1)} %pad_add_fusion.13, ...), channel_id=1, replica_groups=mesh['group'=2,'ctx'=4,'head'=4] {'ctx'}, use_global_device_ids=true, to_apply=%region_26.27 | all-reduce | flops 12384 | bytes 99072 | tf_op jit(solution)/shard_map/psum | solution.py:240
  237.0 1.3 slice_add_fusion
  238.3 3.6 %scatter-add.10 = bf16[256,2048]{0,1:T(8,128)(2,1)S(1)} dynamic-update-slice(bf16[256,2048]{0,1:T(8,128)(2,1)S(1)} %copy-done.17, bf16[3,2048]{0,1:T(8,128)(2,1)S(1)} %slice_add_fusion, s32[]{:T(128)} %constant.194.clone.1, s32[]{:T(128)} %constant.187.clone.1) | dynamic-update-slice | bytes 24580 | tf_op jit(solution)/shard_map/scatter-add | solution.py:233
  241.9 1.4 copy.256
  (316 shorter events, 32.0 us)
Async XLA Ops:
  7.2 57.9 %all-gather.14.cloned.1.call-start = ((), (), s32[]{:S(2)}) async-start(), calls=%async_computation.1 | async-start | bytes 1310720 | tf_op jit(solution)/shard_map/all_gather | solution.py:25
  8.7 15.2 %collective-permute-start = (bf16[3,2560]{1,0:T(4,128)(2,1)S(1)}, bf16[3,2560]{1,0:T(4,128)(2,1)S(1)}, u32[]{:S(2)}, u32[]{:S(2)}) collective-permute-start(bf16[3,2560]{1,0:T(4,128)(2,1)S(1)} %pad_maximum_fusion.4), channel_id=1, source_target_pairs={{0,4},{4,8},{8,12},{1,5},{5,9},{9,13},{2,6},{6,10},{10,14},{3,7},{... | collective-permute-start | bytes 46088 | tf_op jit(solution)/shard_map/ppermute | solution.py:19
  17.1 4.2 %copy-start.11 = (f32[1,256,2,16]{3,2,1,0:T(2,128)}, f32[1,256,2,16]{3,2,1,0:T(2,128)S(1)}, u32[]{:S(2)}) copy-start(f32[1,256,2,16]{3,2,1,0:T(2,128)S(1)} %copy.214) | copy-start | bytes 98308
  17.2 2.7 %copy-start.96 = (f32[2,16]{1,0:T(2,128)}, f32[2,16]{1,0:T(2,128)S(1)}, u32[]{:S(2)}) copy-start(f32[2,16]{1,0:T(2,128)S(1)} %neg.49) | copy-start | bytes 388
  17.6 3.8 %copy-start.63 = (f32[4,2048]{1,0:T(4,128)S(1)}, f32[4,2048]{1,0:T(4,128)}, u32[]{:S(2)}) copy-start(f32[4,2048]{1,0:T(4,128)} %param.25) | copy-start | bytes 98308
  17.6 4.1 %copy-start.83 = (f32[2,4,256]{2,1,0:T(4,128)S(1)}, f32[2,4,256]{2,1,0:T(4,128)}, u32[]{:S(2)}) copy-start(f32[2,4,256]{2,1,0:T(4,128)} %param.26) | copy-start | bytes 24580
  17.6 4.7 %copy-start.31 = (bf16[256,2048]{1,0:T(8,128)(2,1)S(1)}, bf16[256,2048]{1,0:T(8,128)(2,1)}, u32[]{:S(2)}) copy-start(bf16[256,2048]{1,0:T(8,128)(2,1)} %param.21) | copy-start | bytes 3145732
  21.7 5.3 %copy-start.54 = (f32[1,2048]{1,0:T(1,128)}, f32[1,2048]{1,0:T(1,128)S(1)}, u32[]{:S(2)}) copy-start(f32[1,2048]{1,0:T(1,128)S(1)} %get-tuple-element.575) | copy-start | bytes 24580
  21.7 5.3 %copy-start.56 = (f32[1,2048]{1,0:T(1,128)}, f32[1,2048]{1,0:T(1,128)S(1)}, u32[]{:S(2)}) copy-start(f32[1,2048]{1,0:T(1,128)S(1)} %get-tuple-element.576) | copy-start | bytes 24580
  22.8 4.2 %copy-start.8 = (bf16[256,2048]{0,1:T(8,128)(2,1)}, bf16[256,2048]{0,1:T(8,128)(2,1)S(1)}, u32[]{:S(2)}) copy-start(bf16[256,2048]{0,1:T(8,128)(2,1)S(1)} %copy.221) | copy-start | bytes 3145732
  23.9 9.7 %copy-start.1 = (f32[256,2048]{0,1:T(8,128)}, f32[256,2048]{0,1:T(8,128)S(1)}, u32[]{:S(2)}) copy-start(f32[256,2048]{0,1:T(8,128)S(1)} %convert_element_type.286) | copy-start | bytes 6291460
  27.0 6.5 %copy-start.20 = (f32[256,256]{0,1:T(8,128)S(1)}, f32[256,256]{0,1:T(8,128)}, u32[]{:S(2)}) copy-start(f32[256,256]{0,1:T(8,128)} %get-tuple-element.555) | copy-start | bytes 786436
  27.0 6.5 %copy-start.22 = (f32[256,256]{0,1:T(8,128)S(1)}, f32[256,256]{0,1:T(8,128)}, u32[]{:S(2)}) copy-start(f32[256,256]{0,1:T(8,128)} %get-tuple-element.556) | copy-start | bytes 786436
  27.0 6.5 %copy-start.27 = (f32[3,256]{0,1:T(8,128)S(1)}, f32[3,256]{0,1:T(8,128)}, u32[]{:S(2)}) copy-start(f32[3,256]{0,1:T(8,128)} %copy.224) | copy-start | bytes 9220
  27.1 6.5 %copy-start.29 = (f32[3,256]{0,1:T(8,128)S(1)}, f32[3,256]{0,1:T(8,128)}, u32[]{:S(2)}) copy-start(f32[3,256]{0,1:T(8,128)} %copy.225) | copy-start | bytes 9220
  27.1 6.5 %copy-start.66 = (f32[1,1,256]{2,1,0:T(1,128)S(1)}, f32[1,1,256]{2,1,0:T(1,128)}, u32[]{:S(2)}) copy-start(f32[1,1,256]{2,1,0:T(1,128)} %get-tuple-element.579) | copy-start | bytes 3076
  27.1 6.5 %copy-start.68 = (f32[1,1,256]{2,1,0:T(1,128)S(1)}, f32[1,1,256]{2,1,0:T(1,128)}, u32[]{:S(2)}) copy-start(f32[1,1,256]{2,1,0:T(1,128)} %get-tuple-element.580) | copy-start | bytes 3076
  27.1 6.5 %copy-start.70 = (f32[1,1,256]{2,1,0:T(1,128)S(1)}, f32[1,1,256]{2,1,0:T(1,128)}, u32[]{:S(2)}) copy-start(f32[1,1,256]{2,1,0:T(1,128)} %get-tuple-element.585) | copy-start | bytes 3076
  27.1 6.5 %copy-start.72 = (f32[1,1,256]{2,1,0:T(1,128)S(1)}, f32[1,1,256]{2,1,0:T(1,128)}, u32[]{:S(2)}) copy-start(f32[1,1,256]{2,1,0:T(1,128)} %get-tuple-element.586) | copy-start | bytes 3076
  27.1 6.5 %copy-start.74 = (f32[1,1,256]{2,1,0:T(1,128)S(1)}, f32[1,1,256]{2,1,0:T(1,128)}, u32[]{:S(2)}) copy-start(f32[1,1,256]{2,1,0:T(1,128)} %get-tuple-element.581) | copy-start | bytes 3076
  27.1 6.5 %copy-start.76 = (f32[1,1,256]{2,1,0:T(1,128)S(1)}, f32[1,1,256]{2,1,0:T(1,128)}, u32[]{:S(2)}) copy-start(f32[1,1,256]{2,1,0:T(1,128)} %get-tuple-element.582) | copy-start | bytes 3076
  27.1 6.5 %copy-start.78 = (f32[1,1,256]{2,1,0:T(1,128)S(1)}, f32[1,1,256]{2,1,0:T(1,128)}, u32[]{:S(2)}) copy-start(f32[1,1,256]{2,1,0:T(1,128)} %get-tuple-element.583) | copy-start | bytes 3076
  27.1 6.5 %copy-start.80 = (f32[1,1,256]{2,1,0:T(1,128)S(1)}, f32[1,1,256]{2,1,0:T(1,128)}, u32[]{:S(2)}) copy-start(f32[1,1,256]{2,1,0:T(1,128)} %get-tuple-element.584) | copy-start | bytes 3076
  27.2 8.3 %copy-start.47 = (f32[256,2,16]{0,2,1:T(8,128)S(1)}, f32[256,2,16]{0,2,1:T(8,128)}, u32[]{:S(2)}) copy-start(f32[256,2,16]{0,2,1:T(8,128)} %copy.231) | copy-start | bytes 98308
  33.6 87.7 %copy-start.3 = (bf16[256,2048]{0,1:T(8,128)(2,1)}, bf16[256,2048]{0,1:T(8,128)(2,1)S(1)}, u32[]{:S(2)}) copy-start(bf16[256,2048]{0,1:T(8,128)(2,1)S(1)} %get-tuple-element.538) | copy-start | bytes 3145732
  35.4 27.5 %copy-start.24 = (bf16[256,256]{0,1:T(8,128)(2,1)}, bf16[256,256]{0,1:T(8,128)(2,1)S(1)}, u32[]{:S(2)}) copy-start(bf16[256,256]{0,1:T(8,128)(2,1)S(1)} %get-tuple-element.540) | copy-start | bytes 393220
  35.4 20.3 %copy-start.32 = (f32[256,2,16]{2,1,0:T(2,128)S(1)}, f32[256,2,16]{2,1,0:T(2,128)}, u32[]{:S(2)}) copy-start(f32[256,2,16]{2,1,0:T(2,128)} %get-tuple-element.536) | copy-start | bytes 98308
  35.4 21.0 %copy-start.99 = (f32[32]{0:T(128)S(1)}, f32[32]{0:T(128)}, u32[]{:S(2)}) copy-start(f32[32]{0:T(128)} %get-tuple-element.493) | copy-start | bytes 388
  36.7 57.4 %all-gather.12.cloned.1.call-start = ((), (), s32[]{:S(2)}) async-start(), calls=%async_computation | async-start | bytes 1310720 | tf_op jit(solution)/shard_map/all_gather | solution.py:25
  62.9 109.3 %all-gather.16.cloned.1.call-start = ((), (), s32[]{:S(2)}) async-start(), calls=%async_computation.2 | async-start | bytes 2621440 | tf_op jit(solution)/shard_map/all_gather | solution.py:48
  99.2 3.5 %copy-start.14 = (f32[2,16,64,256]{3,2,1,0:T(8,128)}, f32[2,16,64,256]{3,2,1,0:T(8,128)S(1)}, u32[]{:S(2)}) copy-start(f32[2,16,64,256]{3,2,1,0:T(8,128)S(1)} %fusion.95) | copy-start | bytes 6291460
  99.9 2.8 %copy-start.5 = (bf16[256,2048]{0,1:T(8,128)(2,1)S(1)}, bf16[256,2048]{0,1:T(8,128)(2,1)}, u32[]{:S(2)}) copy-start(bf16[256,2048]{0,1:T(8,128)(2,1)} %copy.235) | copy-start | bytes 3145732
  102.7 12.3 %copy-start = (f32[1,256,2,16,64]{1,4,3,2,0:T(8,128)}, f32[1,256,2,16,64]{1,4,3,2,0:T(8,128)S(1)}, u32[]{:S(2)}) copy-start(f32[1,256,2,16,64]{1,4,3,2,0:T(8,128)S(1)} %fusion.32) | copy-start | bytes 6291460
  111.4 3.6 %copy-start.82 = (f32[256]{0:T(256)}, f32[256]{0:T(256)S(1)}, u32[]{:S(2)}) copy-start(f32[256]{0:T(256)S(1)} %add_rsqrt_fusion) | copy-start | bytes 3076
  121.3 4.9 %copy-start.46 = (f32[256,2,16]{0,2,1:T(8,128)S(1)}, f32[256,2,16]{0,2,1:T(8,128)}, u32[]{:S(2)}) copy-start(f32[256,2,16]{0,2,1:T(8,128)} %copy.234) | copy-start | bytes 98308
  121.3 4.9 %copy-start.86 = (f32[2,16]{1,0:T(2,128)S(1)}, f32[2,16]{1,0:T(2,128)}, u32[]{:S(2)}) copy-start(f32[2,16]{1,0:T(2,128)} %exponential_multiply_fusion) | copy-start | bytes 388
  160.9 3.5 %copy-start.25 = (bf16[256,256]{0,1:T(8,128)(2,1)S(1)}, bf16[256,256]{0,1:T(8,128)(2,1)}, u32[]{:S(2)}) copy-start(bf16[256,256]{0,1:T(8,128)(2,1)} %copy-done.24) | copy-start | bytes 393220
  160.9 3.5 %copy-start.33 = (bf16[2,256,256]{2,1,0:T(8,128)(2,1)S(1)}, bf16[2,256,256]{2,1,0:T(8,128)(2,1)}, u32[]{:S(2)}) copy-start(bf16[2,256,256]{2,1,0:T(8,128)(2,1)} %get-tuple-element.475) | copy-start | bytes 786436
  189.1 3.3 %copy-start.2 = (f32[256,2048]{0,1:T(8,128)S(1)}, f32[256,2048]{0,1:T(8,128)}, u32[]{:S(2)}) copy-start(f32[256,2048]{0,1:T(8,128)} %copy-done.1) | copy-start | bytes 6291460
  189.1 3.3 %copy-start.9 = (bf16[256,2048]{0,1:T(8,128)(2,1)S(1)}, bf16[256,2048]{0,1:T(8,128)(2,1)}, u32[]{:S(2)}) copy-start(bf16[256,2048]{0,1:T(8,128)(2,1)} %copy-done.8) | copy-start | bytes 3145732
  189.1 3.3 %copy-start.10 = (f32[3,2048]{0,1:T(8,128)S(1)}, f32[3,2048]{0,1:T(8,128)}, u32[]{:S(2)}) copy-start(f32[3,2048]{0,1:T(8,128)} %copy.222) | copy-start | bytes 73732
  189.1 3.3 %copy-start.13 = (f32[256,2048]{0,1:T(8,128)S(1)}, f32[256,2048]{0,1:T(8,128)}, u32[]{:S(2)}) copy-start(f32[256,2048]{0,1:T(8,128)} %get-tuple-element.539) | copy-start | bytes 6291460
  192.5 4.2 %copy-start.55 = (f32[1,2048]{1,0:T(1,128)S(1)}, f32[1,2048]{1,0:T(1,128)}, u32[]{:S(2)}) copy-start(f32[1,2048]{1,0:T(1,128)} %copy-done.54) | copy-start | bytes 24580
  192.5 4.2 %copy-start.57 = (f32[1,2048]{1,0:T(1,128)S(1)}, f32[1,2048]{1,0:T(1,128)}, u32[]{:S(2)}) copy-start(f32[1,2048]{1,0:T(1,128)} %copy-done.56) | copy-start | bytes 24580
  201.0 2.4 copy-start.35
  201.0 2.4 copy-start.36
  203.0 6.5 %copy-start.34 = (f32[2,16,256]{1,0,2:T(2,128)S(1)}, f32[2,16,256]{1,0,2:T(2,128)}, u32[]{:S(2)}) copy-start(f32[2,16,256]{1,0,2:T(2,128)} %copy.244) | copy-start | bytes 98308
  203.0 6.5 %copy-start.97 = (f32[2,16]{1,0:T(2,128)S(1)}, f32[2,16]{1,0:T(2,128)}, u32[]{:S(2)}) copy-start(f32[2,16]{1,0:T(2,128)} %copy-done.96) | copy-start | bytes 388
  203.5 6.5 %copy-start.50 = (f32[256,32]{0,1:T(8,128)S(1)}, f32[256,32]{0,1:T(8,128)}, u32[]{:S(2)}) copy-start(f32[256,32]{0,1:T(8,128)} %param.24) | copy-start | bytes 98308
  203.5 6.5 %copy-start.85 = (f32[32]{0:T(128)S(1)}, f32[32]{0:T(128)}, u32[]{:S(2)}) copy-start(f32[32]{0:T(128)} %copy-done.84) | copy-start | bytes 388
  203.5 8.2 %slice-start = ((f32[259,2048]{0,1:T(8,128)}), f32[3,2048]{0,1:T(8,128)S(1)}, s32[]{:S(2)}) async-start(f32[259,2048]{0,1:T(8,128)} %copy-done.7), calls=%async_computation.3 | async-start | bytes 2097152 | tf_op jit(solution)/shard_map/transpose(jvp())/split | solution.py:137
  203.5 8.2 %copy-start.41 = (f32[3,256]{0,1:T(8,128)S(1)}, f32[3,256]{0,1:T(8,128)}, u32[]{:S(2)}) copy-start(f32[3,256]{0,1:T(8,128)} %pad_add_fusion.9) | copy-start | bytes 9220
  210.0 3.5 %copy-start.92 = (f32[256]{0:T(256)S(1)}, f32[256]{0:T(256)}, u32[]{:S(2)}) copy-start(f32[256]{0:T(256)} %get-tuple-element.485) | copy-start | bytes 3076
  210.0 3.5 %copy-start.93 = (f32[256]{0:T(256)S(1)}, f32[256]{0:T(256)}, u32[]{:S(2)}) copy-start(f32[256]{0:T(256)} %get-tuple-element.490) | copy-start | bytes 3076
  210.0 3.5 %copy-start.94 = (f32[256]{0:T(256)S(1)}, f32[256]{0:T(256)}, u32[]{:S(2)}) copy-start(f32[256]{0:T(256)} %get-tuple-element.491) | copy-start | bytes 3076
  210.0 3.5 %copy-start.95 = (f32[256]{0:T(256)S(1)}, f32[256]{0:T(256)}, u32[]{:S(2)}) copy-start(f32[256]{0:T(256)} %get-tuple-element.492) | copy-start | bytes 3076
  210.0 3.6 %copy-start.88 = (f32[256]{0:T(256)S(1)}, f32[256]{0:T(256)}, u32[]{:S(2)}) copy-start(f32[256]{0:T(256)} %get-tuple-element.486) | copy-start | bytes 3076
  210.0 3.6 %copy-start.89 = (f32[256]{0:T(256)S(1)}, f32[256]{0:T(256)}, u32[]{:S(2)}) copy-start(f32[256]{0:T(256)} %get-tuple-element.487) | copy-start | bytes 3076
  210.1 3.6 %copy-start.90 = (f32[256]{0:T(256)S(1)}, f32[256]{0:T(256)}, u32[]{:S(2)}) copy-start(f32[256]{0:T(256)} %get-tuple-element.488) | copy-start | bytes 3076
  210.1 3.6 %copy-start.91 = (f32[256]{0:T(256)S(1)}, f32[256]{0:T(256)}, u32[]{:S(2)}) copy-start(f32[256]{0:T(256)} %get-tuple-element.489) | copy-start | bytes 3076
  210.1 3.6 %copy-start.18 = (f32[1,256,256]{1,2,0:T(8,128)S(1)}, f32[1,256,256]{1,2,0:T(8,128)}, u32[]{:S(2)}) copy-start(f32[1,256,256]{1,2,0:T(8,128)} %fusion.88) | copy-start | bytes 786436
  210.1 3.6 %copy-start.19 = (f32[1,256,256]{1,2,0:T(8,128)S(1)}, f32[1,256,256]{1,2,0:T(8,128)}, u32[]{:S(2)}) copy-start(f32[1,256,256]{1,2,0:T(8,128)} %fusion.87) | copy-start | bytes 786436
  212.2 21.9 %collective-permute-start.1 = (f32[3,2560]{1,0:T(4,128)S(1)}, f32[3,2560]{1,0:T(4,128)S(1)}, u32[]{:S(2)}, u32[]{:S(2)}) collective-permute-start(f32[3,2560]{1,0:T(4,128)S(1)} %copy.239), channel_id=1, source_target_pairs={{4,0},{8,4},{12,8},{5,1},{9,5},{13,9},{6,2},{10,6},{14,10},{7,3},{... | collective-permute-start | bytes 92168 | tf_op jit(solution)/shard_map/ppermute | solution.py:19
  235.7 2.6 %copy-start.17 = (bf16[256,2048]{0,1:T(8,128)(2,1)S(1)}, bf16[256,2048]{0,1:T(8,128)(2,1)}, u32[]{:S(2)}) copy-start(bf16[256,2048]{0,1:T(8,128)(2,1)} %split.24) | copy-start | bytes 3145732
  (44 other events, 73.8 us)
Sparse Core Ops, SparseCore 0:
  36.8 28.2 all-gather.13
  66.7 27.3 all-gather.11
  127.6 44.6 all-gather.15
where the time goes:
time: 252 us; the launch traced here: 250 us
  other arithmetic  70 us (28%)
  blocking collectives  61 us (24%)
  local copies, waits for them, and re-layouts  41.1 us (16%)
  waiting for transfers between devices  32.5 us (13%)
  matrix products  23.3 us (9%)
  between operations  15.4 us (6%)
  starting transfers between devices  6.37 us (3%)
    all_gather x2, waiting for transfers between devices, entering_2(): lax.all_gather(part.astype(kind), axis)  25.6 us
    psum x1, blocking collectives, shards(): lax.psum((gradients[4], gradients[5], gradients[6], grad_gain_own), 'ctx')  20.3 us
    all_gather x2, blocking collectives, entering_2(): lax.all_gather(part.astype(kind), axis)  17.6 us
    dot_general x3, matrix products, span_parts(): jnp.einsum('gkts,sgkp->tgkp', mixing, x_block, preferred_element_type=jnp...  14.3 us
    unnamed x214, local copies, waits for them, and re-layouts  13.1 us
    all_gather x1, blocking collectives, prefix(): lax.all_gather(part.astype(kind), axis)  9.92 us
    select_n x8, other arithmetic, entering_step(): return jax.tree.map(lambda a, b: jnp.where(reached, a, b), new, before)  8.73 us
    convert_element_type x2, other arithmetic, conv_silu(): return jax.nn.silu(summed).astype(jnp.bfloat16)  8.12 us
  transfers between devices with their start and end apart: 5, of which 3 were waited for; matrix products, arithmetic and copies ran while one was open for 21% of the time, Pallas kernels for 0%

commit v1 on v0

--- a/solution.py
+++ b/solution.py
@@ -1,7 +1,9 @@
+import functools
 import jax
 import jax.numpy as jnp
 from jax import lax
 from jax.sharding import PartitionSpec as P
+from jax.lax import all_gather
 
 HEADS = 128
 HEAD_DIM = 64
@@ -11,6 +13,13 @@
 SPAN = 256
 INNER = 8192
 epsilon = 1e-05
+
+
+def match_sides(local_block, bus_axis):
+    return jnp.sum(all_gather(local_block, axis_name=bus_axis), axis=0)
+
+
+counts_try_all = functools.partial(match_sides, bus_axis="head")
 
 
 def passed_along(shard, axis, by):
@@ -199,7 +208,7 @@
     square = lax.psum(own_square, "head")
     factor = lax.rsqrt(square / INNER + epsilon)
     normed = gated * factor[:, None]
-    projected = lax.psum(jnp.sum(upstream * normed, axis=1), "head")
+    projected = counts_try_all(jnp.sum(upstream * normed, axis=1))
     d_gated = (upstream - normed * (projected / INNER)[:, None]) * factor[:, None]
     grad_gain_own = jnp.sum(grad_output.astype(jnp.float32) * normed, axis=0)
     d_mixed = d_gated * gate_act

time: 252 us -> 272 us (1.079)
  local copies, waits for them, and re-layouts: 41.1 us -> 51.3 us
  other arithmetic: 70 us -> 79.8 us
    psum x1 -> x0, blocking collectives: 6.33 us -> none  [shards(): projected = lax.psum(jnp.sum(upstream * normed, axis=1), 'head')]
    all_gather x0 -> x1, blocking collectives: none -> 5.23 us  [match_sides(): return jnp.sum(all_gather(local_block, axis_name=bus_axis), axis=0)]
    unnamed x214 -> x218, local copies, waits for them, and re-layouts: 13.1 us -> 15 us
  transfers between devices with their start and end apart: 5 -> 5, of which waited for: 3 -> 3; matrix products, arithmetic and copies ran while one was open for 21% -> 20% of each run, Pallas kernels for 0% -> 0%
where the time goes in v1:
time: 272 us; the launch traced here: 269 us
  other arithmetic  79.8 us (29%)
  blocking collectives  61.2 us (22%)
  local copies, waits for them, and re-layouts  51.3 us (19%)
  waiting for transfers between devices  32 us (12%)
  matrix products  23.3 us (9%)
  between operations  15.2 us (6%)
  starting transfers between devices  6.37 us (2%)
    all_gather x2, waiting for transfers between devices, entering_2(): lax.all_gather(part.astype(kind), axis)  25.6 us
    psum x1, blocking collectives, shards(): lax.psum((gradients[4], gradients[5], gradients[6], grad_gain_own), 'ctx')  20.8 us
    all_gather x2, blocking collectives, entering_2(): lax.all_gather(part.astype(kind), axis)  17.6 us
    unnamed x218, local copies, waits for them, and re-layouts  15 us
    dot_general x3, matrix products, span_parts(): jnp.einsum('gkts,sgkp->tgkp', mixing, x_block, preferred_element_type=jnp...  14.3 us
    all_gather x1, blocking collectives, prefix(): lax.all_gather(part.astype(kind), axis)  10.8 us
    select_n x8, other arithmetic, entering_step(): return jax.tree.map(lambda a, b: jnp.where(reached, a, b), new, before)  8.73 us
    convert_element_type x2, other arithmetic, conv_silu(): return jax.nn.silu(summed).astype(jnp.bfloat16)  8.1 us
  transfers between devices with their start and end apart: 5, of which 3 were waited for; matrix products, arithmetic and copies ran while one was open for 20% of the time, Pallas kernels for 0%

profile of v1, /device:TPU:0, one launch (start us, length us, event | category | flops | bytes accessed | tf_op | source)
XLA Modules:
  0.0 269.4 jit_solution(12102898184971824187)
XLA Ops:
  8.7 5.0 %collective-permute-start = (bf16[3,2560]{1,0:T(4,128)(2,1)S(1)}, bf16[3,2560]{1,0:T(4,128)(2,1)S(1)}, u32[]{:S(2)}, u32[]{:S(2)}) collective-permute-start(bf16[3,2560]{1,0:T(4,128)(2,1)S(1)} %pad_maximum_fusion.4), channel_id=1, source_target_pairs={{0,4},{4,8},{8,12},{1,5},{5,9},{9,13},{2,6},{6,10},{10,14},{3,7},{... | collective-permute-start | bytes 46088 | tf_op jit(solution)/shard_map/ppermute | solution.py:28
  14.8 1.3 slice_reduce_fusion
  17.7 1.2 reduce-window.14
  26.4 1.3 copy.222
  27.9 6.4 %multiply_convert_fusion.5 = (bf16[256,2048]{0,1:T(8,128)(2,1)S(1)}, f32[256,2048]{0,1:T(8,128)}) fusion(f32[256,2048]{0,1:T(8,128)S(1)} %convert_element_type.286, f32[2048]{0:T(1024)S(1)} %bitcast.393, f32[3,2048]{0,1:T(8,128)} %copy.222, f32[2048]{0:T(1024)S(1)} %bitcast.395, f32[2048]{0:T(1024)S(1)} %bitcast.397, f32[2048]{0:T(1024)S(1)} %bitcast.391), kind=kLoop, calls=%fused_computation.81 | loop fusion | flops 7864320 | bytes 5300224 | tf_op jit(solution)/shard_map/jvp()/convert_element_type | solution.py:84
  34.4 1.7 multiply_convert_fusion.16
  38.1 9.1 %all-gather.8 = bf16[4,2,8]{2,1,0:T(2,128)(2,1)S(1)} all-gather(bf16[1,2,8]{2,1,0:T(2,128)(2,1)S(1)} %get-tuple-element.588), channel_id=5, replica_groups=mesh['group'=2,'ctx'=4,'head'=4] {'ctx'}, dimensions={0}, use_global_device_ids=true | all-gather | bytes 160 | tf_op jit(solution)/shard_map/all_gather | solution.py:34
  47.2 8.5 %all-gather.7 = bf16[4,2,8]{2,1,0:T(2,128)(2,1)S(1)} all-gather(bf16[1,2,8]{2,1,0:T(2,128)(2,1)S(1)} %get-tuple-element.589), channel_id=3, replica_groups=mesh['group'=2,'ctx'=4,'head'=4] {'ctx'}, dimensions={0}, use_global_device_ids=true | all-gather | bytes 160 | tf_op jit(solution)/shard_map/all_gather | solution.py:34
  57.8 2.3 copy.235
  60.1 2.3 copy.220
  64.7 1.1 all-gather.16.cloned.1.call-done
  65.8 4.5 %while.48 = (s32[]{:T(128)}, f32[2,8,64,128]{3,2,1,0:T(8,128)S(1)}, s32[]{:T(128)}, bf16[4,2,8]{2,1,0:T(2,128)(2,1)S(1)}, bf16[4,2,8,64,128]{4,3,2,1,0:T(8,128)(2,1)}, /*index=5*/s32[]{:T(128)}, s32[]{:T(128)}) while((s32[]{:T(128)}, f32[2,8,64,128]{3,2,1,0:T(8,128)S(1)}, s32[]{:T(128)}, bf16[4,2,8]{2,1,0:T(2,128)(2,1)S(1)}, ...), condition=%wide.region_5.6_spmd.clone, body=%wide.region_4.5_spmd.clone.sunk | while | flops 655380 | bytes 1310985 | solution.py:51
  65.8 1.1 fusion.145
  68.1 1.1 fusion.145
  70.3 24.5 %all-gather.14.cloned.1.call-done = bf16[8,8,64,128]{3,2,1,0:T(8,128)(2,1)} async-done(((bf16[2,8,64,128]{3,2,1,0:T(8,128)(2,1)}), bf16[8,8,64,128]{3,2,1,0:T(8,128)(2,1)}) %all-gather.14.cloned.1.call-update) | async-done | bytes 1048592 | tf_op jit(solution)/shard_map/all_gather | solution.py:34
  94.8 4.5 %while.47 = (s32[]{:T(128)}, f32[2,8,64,128]{3,2,1,0:T(8,128)S(1)}, s32[]{:T(128)}, bf16[4,2,8]{2,1,0:T(2,128)(2,1)S(1)}, bf16[4,2,8,64,128]{4,3,2,1,0:T(8,128)(2,1)}, /*index=5*/s32[]{:T(128)}, s32[]{:T(128)}) while((s32[]{:T(128)}, f32[2,8,64,128]{3,2,1,0:T(8,128)S(1)}, s32[]{:T(128)}, bf16[4,2,8]{2,1,0:T(2,128)(2,1)S(1)}, ...), condition=%wide.region_3.4_spmd.clone, body=%wide.region_2.3_spmd.clone.sunk | while | flops 655380 | bytes 1310985 | solution.py:51
  94.8 1.1 fusion.144
  100.6 2.8 %fusion.32 = f32[1,256,2,16,64]{1,4,3,2,0:T(8,128)S(1)} fusion(f32[2,16,64,256]{3,2,1,0:T(8,128)S(1)} %fusion.95, bf16[256,2,16,64]{0,3,2,1:T(8,128)(2,1)S(1)} %bitcast.360, f32[2,16,256]{2,1,0:T(8,128)S(1)} %bitcast.387, f32[2,16,256]{2,1,0:T(8,128)S(1)} %copy-done.61, f32[2,256,256]{2,1,0:T(8,128)S(1)} %copy-done.39, pred[256,256]{1,0:T(8,128)(4,1)S(1)} %copy-done.54, ...), kind=kOutput, calls=%fused_computation.58 | convolution fusion | flops 283639808 | bytes 6979712 | tf_op jit(solution)/shard_map/jvp(vmap(gkts,sgkp->tgkp))/dot_general | solution.py:98
  103.4 1.3 multiply_reduce_fusion.5
  104.7 6.7 %psum.35 = f32[256]{0:T(256)} all-reduce(f32[256]{0:T(256)} %multiply_reduce_fusion.5), channel_id=1, replica_groups=mesh['group'=2,'ctx'=4,'head'=4] {'head'}, use_global_device_ids=true, to_apply=%region_7.8 | all-reduce | flops 256 | bytes 2048 | tf_op jit(solution)/shard_map/psum | solution.py:208
  112.1 3.6 %fusion.20 = (f32[2048]{0:T(1024)}, f32[256]{0:T(256)S(1)}) fusion(bf16[256,2048]{0,1:T(8,128)(2,1)} %copy.220, f32[256]{0:T(256)S(1)} %add_rsqrt_fusion, bf16[256,2048]{0,1:T(8,128)(2,1)} %copy.235, f32[1,256,2,16,64]{1,4,3,2,0:T(8,128)S(1)} %fusion.32, f32[2048]{0:T(1024)} %param.28), kind=kLoop, calls=%fused_computation.44 | loop fusion | flops 6813440 | bytes 4212736 | tf_op jit(solution)/shard_map/reduce_sum | solution.py:213
  115.7 5.2 %all-gather.9 = f32[4,1,256]{2,1,0:T(1,128)S(1)} all-gather(f32[1,1,256]{2,1,0:T(1,128)S(1)} %bitcast.431), channel_id=7, replica_groups=mesh['group'=2,'ctx'=4,'head'=4] {'head'}, dimensions={0}, use_global_device_ids=true | all-gather | bytes 5120 | tf_op jit(solution)/shard_map/all_gather | solution.py:19
  121.0 4.8 %multiply_reduce_fusion = (f32[2048]{0:T(1024)}, f32[256,2048]{0,1:T(8,128)S(1)}, bf16[256,2048]{0,1:T(8,128)(2,1)}) fusion(bf16[256,2048]{0,1:T(8,128)(2,1)S(1)} %get-tuple-element.538, f32[256]{0:T(256)S(1)} %broadcast_multiply_fusion.13, f32[256]{0:T(256)} %copy-done.82, bf16[256,2048]{0,1:T(8,128)(2,1)} %copy.235, f32[1,256,2,16,64]{1,4,3,2,0:T(8,128)} %copy-done, ...), kind=kLoop, calls=%fused_computation.73 | loop fusion | flops 12056576 | bytes 8407040 | tf_op jit(solution)/shard_map/transpose(jvp(vmap()))/reduce_sum | solution.py:99
  125.9 1.2 fusion.56
  127.1 10.8 %all-gather = bf16[4,1,2,16]{3,2,1,0:T(2,128)(2,1)} all-gather(bf16[1,1,2,16]{3,2,1,0:T(2,128)(2,1)} %get-tuple-element.567), channel_id=2, replica_groups=mesh['group'=2,'ctx'=4,'head'=4] {'ctx'}, dimensions={0}, use_global_device_ids=true | all-gather | bytes 320 | tf_op jit(solution)/shard_map/all_gather | solution.py:57
  137.9 2.6 fusion.33
  140.5 1.6 copy.245
  142.1 8.2 %fusion.13 = (f32[2,16,256]{2,1,0:T(8,128)}, f32[2,16,256]{2,1,0:T(8,128)}, f32[2,16,256]{2,1,0:T(8,128)}, bf16[2,256,256]{2,1,0:T(8,128)(2,1)}) fusion(f32[2,16,256]{2,1,0:T(8,128)} %bitcast.386, f32[2,16,256]{2,1,0:T(8,128)} %copy.228, f32[2,256,256]{2,1,0:T(8,128)} %fusion.124, pred[256,256]{1,0:T(8,128)(4,1)} %iota_compare_fusion, ...), kind=kOutput, calls=%fused_computation.23 | convolution fusion | flops 301834240 | bytes 4161536 | tf_op jit(solution)/shard_map/transpose(jvp(vmap(gkts,sgkp->tgkp)))/dot_general | solution.py:98
  150.3 1.6 copy.247
  151.9 1.6 copy.248
  153.5 1.6 copy.244
  155.1 1.4 reduce_sum.301
  156.5 1.4 reduce_sum.302
  157.8 1.2 reshape.695
  159.1 2.3 copy.258
  161.3 1.9 fusion.70
  163.2 1.6 fusion.63
  165.8 6.4 %all-gather.18.cloned.1.call-done = bf16[8,16,64,128]{3,2,1,0:T(8,128)(2,1)} async-done(((bf16[2,16,64,128]{3,2,1,0:T(8,128)(2,1)}), bf16[8,16,64,128]{3,2,1,0:T(8,128)(2,1)}) %all-gather.18.cloned.1.call-update) | async-done | bytes 2097168 | tf_op jit(solution)/shard_map/all_gather | solution.py:57
  172.1 7.7 %while.49 = (s32[]{:T(128)}, f32[2,16,64,128]{3,2,1,0:T(8,128)S(1)}, s32[]{:T(128)}, bf16[4,2,16]{2,1,0:T(2,128)(2,1)}, bf16[4,2,16,64,128]{4,3,2,1,0:T(8,128)(2...) while((s32[]{:T(128)}, f32[2,16,64,128]{3,2,1,0:T(8,128)S(1)}, s32[]{:T(128)}, ...), condition=%wide.region_11.12_spmd.clone, body=%wide.region_10.11_spmd.clone.sunk | while | flops 1310760 | bytes 2621927 | solution.py:75
  172.7 1.3 fusion.146
  174.7 1.3 fusion.146
  176.6 1.3 fusion.146
  178.5 1.3 fusion.146
  179.9 2.1 multiply_reduce_fusion.6
  183.6 1.7 multiply_reduce_fusion.14
  188.8 3.3 %fusion.59 = bf16[1,256,2,16,64]{1,4,3,2,0:T(8,128)(2,1)S(1)} fusion(f32[2,16,64,256]{3,2,1,0:T(8,128)S(1)} %bitcast.357, f32[2,16,256]{2,1,0:T(8,128)S(1)} %bitcast.388, f32[2,16,256]{2,1,0:T(8,128)S(1)} %copy-done.62, f32[2,256,256]{2,1,0:T(8,128)S(1)} %copy-done.40, pred[256,256]{1,0:T(8,128)(4,1)S(1)} %copy-done.55, ...), kind=kOutput, calls=%fused_computation.96 | convolution fusion | flops 284688384 | bytes 6979712 | tf_op jit(solution)/shard_map/transpose(jvp(vmap(gkts,sgkp->tgkp)))/dot_general | solution.py:98
  192.1 4.7 %multiply_reduce_fusion.3 = (f32[2048]{0:T(1024)}, f32[2048]{0:T(1024)}, f32[2048]{0:T(1024)}, f32[2048]{0:T(1024)}, f32[256,2048]{0,1:T(8,128)S(1)}) fusion(f32[256,2048]{0,1:T(8,128)S(1)} %copy-done.2, f32[3,2048]{0,1:T(8,128)S(1)} %copy-done.11, bf16[256,2048]{0,1:T(8,128)(2,1)S(1)} %copy-done.10, f32[256,2048]{0,1:T(8,128)S(1)} %copy-done.14, ...), kind=kLoop, calls=%fused_computation.76 | loop fusion | flops 11526144 | bytes 8445952 | tf_op jit(solution)/shard_map/transpose(jvp())/reduce_sum | solution.py:83
  196.9 1.8 broadcast_multiply_fusion.3
  198.7 2.5 pad_add_fusion
  201.2 1.7 split.24
  204.1 1.2 fusion.111
  205.4 1.8 fusion.89
  207.3 5.0 %reduce-window.16 = f32[1,16,2,2,128]{4,1,2,3,0:T(8,128)S(1)} reduce-window(f32[1,16,2,2,128]{4,1,2,3,0:T(8,128)S(1)} %copy.249, f32[]{:T(128)} %constant.188.clone.1), window={size=1x1x1x1x128 pad=0_0x0_0x0_0x0_0x0_127}, to_apply=%region_20.21 | reduce-window | flops 1040384 | bytes 65540 | tf_op jit(solution)/shard_map/reduce-window.2
  213.3 1.3 fusion.113
  214.7 1.3 fusion.107
  216.5 1.3 collective-permute-start.1
  220.9 20.8 %all-reduce.35 = (f32[4,2048]{1,0:T(4,128)}, f32[2,4,256]{2,1,0:T(4,128)}, f32[3,32]{1,0:T(4,128)}, f32[2048]{0:T(1024)}) all-reduce(f32[4,2048]{1,0:T(4,128)S(1)} %pad_add_fusion.11, f32[2,4,256]{2,1,0:T(4,128)} %pad_add_fusion.12, f32[3,32]{1,0:T(4,128)} %pad_add_fusion.13, ...), channel_id=1, replica_groups=mesh['group'=2,'ctx'=4,'head'=4] {'ctx'}, use_global_device_ids=true, to_apply=%region_26.27 | all-reduce | flops 12384 | bytes 99072 | tf_op jit(solution)/shard_map/psum | solution.py:249
  243.3 1.8 fusion.100
  245.1 1.7 scatter-add.11
  246.8 1.7 scatter-add.14
  251.1 1.3 copy.240
  252.4 2.1 slice_add_fusion
  254.5 6.1 %scatter-add.10 = bf16[256,2048]{0,1:T(8,128)(2,1)} dynamic-update-slice(bf16[256,2048]{0,1:T(8,128)(2,1)} %split.24, bf16[3,2048]{0,1:T(8,128)(2,1)} %slice_add_fusion, s32[]{:T(128)} %constant.194.clone.1, s32[]{:T(128)} %constant.187.clone.1) | dynamic-update-slice | bytes 24580 | tf_op jit(solution)/shard_map/scatter-add | solution.py:242
  260.6 2.3 copy.256
  (321 shorter events, 43.7 us)
Async XLA Ops:
  7.2 58.7 %all-gather.16.cloned.1.call-start = ((), (), s32[]{:S(2)}) async-start(), calls=%async_computation.1 | async-start | bytes 1310720 | tf_op jit(solution)/shard_map/all_gather | solution.py:34
  8.7 15.9 %collective-permute-start = (bf16[3,2560]{1,0:T(4,128)(2,1)S(1)}, bf16[3,2560]{1,0:T(4,128)(2,1)S(1)}, u32[]{:S(2)}, u32[]{:S(2)}) collective-permute-start(bf16[3,2560]{1,0:T(4,128)(2,1)S(1)} %pad_maximum_fusion.4), channel_id=1, source_target_pairs={{0,4},{4,8},{8,12},{1,5},{5,9},{9,13},{2,6},{6,10},{10,14},{3,7},{... | collective-permute-start | bytes 46088 | tf_op jit(solution)/shard_map/ppermute | solution.py:28
  17.1 5.0 %copy-start.12 = (f32[1,256,2,16]{3,2,1,0:T(2,128)}, f32[1,256,2,16]{3,2,1,0:T(2,128)S(1)}, u32[]{:S(2)}) copy-start(f32[1,256,2,16]{3,2,1,0:T(2,128)S(1)} %copy.214) | copy-start | bytes 98308
  17.2 3.4 %copy-start.96 = (f32[2,16]{1,0:T(2,128)}, f32[2,16]{1,0:T(2,128)S(1)}, u32[]{:S(2)}) copy-start(f32[2,16]{1,0:T(2,128)S(1)} %neg.49) | copy-start | bytes 388
  17.6 4.5 %copy-start.63 = (f32[4,2048]{1,0:T(4,128)S(1)}, f32[4,2048]{1,0:T(4,128)}, u32[]{:S(2)}) copy-start(f32[4,2048]{1,0:T(4,128)} %param.25) | copy-start | bytes 98308
  17.6 4.8 %copy-start.83 = (f32[2,4,256]{2,1,0:T(4,128)S(1)}, f32[2,4,256]{2,1,0:T(4,128)}, u32[]{:S(2)}) copy-start(f32[2,4,256]{2,1,0:T(4,128)} %param.26) | copy-start | bytes 24580
  17.6 5.4 %copy-start.31 = (bf16[256,2048]{1,0:T(8,128)(2,1)S(1)}, bf16[256,2048]{1,0:T(8,128)(2,1)}, u32[]{:S(2)}) copy-start(bf16[256,2048]{1,0:T(8,128)(2,1)} %param.21) | copy-start | bytes 3145732
  22.4 5.4 %copy-start.50 = (f32[1,2048]{1,0:T(1,128)}, f32[1,2048]{1,0:T(1,128)S(1)}, u32[]{:S(2)}) copy-start(f32[1,2048]{1,0:T(1,128)S(1)} %get-tuple-element.575) | copy-start | bytes 24580
  22.4 5.4 %copy-start.52 = (f32[1,2048]{1,0:T(1,128)}, f32[1,2048]{1,0:T(1,128)S(1)}, u32[]{:S(2)}) copy-start(f32[1,2048]{1,0:T(1,128)S(1)} %get-tuple-element.576) | copy-start | bytes 24580
  23.6 4.2 %copy-start.9 = (bf16[256,2048]{0,1:T(8,128)(2,1)}, bf16[256,2048]{0,1:T(8,128)(2,1)S(1)}, u32[]{:S(2)}) copy-start(bf16[256,2048]{0,1:T(8,128)(2,1)S(1)} %copy.221) | copy-start | bytes 3145732
  24.6 9.7 %copy-start.1 = (f32[256,2048]{0,1:T(8,128)}, f32[256,2048]{0,1:T(8,128)S(1)}, u32[]{:S(2)}) copy-start(f32[256,2048]{0,1:T(8,128)S(1)} %convert_element_type.286) | copy-start | bytes 6291460
  27.8 6.5 %copy-start.20 = (f32[256,256]{0,1:T(8,128)S(1)}, f32[256,256]{0,1:T(8,128)}, u32[]{:S(2)}) copy-start(f32[256,256]{0,1:T(8,128)} %get-tuple-element.555) | copy-start | bytes 786436
  27.8 6.5 %copy-start.22 = (f32[256,256]{0,1:T(8,128)S(1)}, f32[256,256]{0,1:T(8,128)}, u32[]{:S(2)}) copy-start(f32[256,256]{0,1:T(8,128)} %get-tuple-element.556) | copy-start | bytes 786436
  27.8 6.5 %copy-start.27 = (f32[3,256]{0,1:T(8,128)S(1)}, f32[3,256]{0,1:T(8,128)}, u32[]{:S(2)}) copy-start(f32[3,256]{0,1:T(8,128)} %copy.224) | copy-start | bytes 9220
  27.8 6.5 %copy-start.29 = (f32[3,256]{0,1:T(8,128)S(1)}, f32[3,256]{0,1:T(8,128)}, u32[]{:S(2)}) copy-start(f32[3,256]{0,1:T(8,128)} %copy.225) | copy-start | bytes 9220
  27.8 6.5 %copy-start.66 = (f32[1,1,256]{2,1,0:T(1,128)S(1)}, f32[1,1,256]{2,1,0:T(1,128)}, u32[]{:S(2)}) copy-start(f32[1,1,256]{2,1,0:T(1,128)} %get-tuple-element.579) | copy-start | bytes 3076
  27.8 6.5 %copy-start.68 = (f32[1,1,256]{2,1,0:T(1,128)S(1)}, f32[1,1,256]{2,1,0:T(1,128)}, u32[]{:S(2)}) copy-start(f32[1,1,256]{2,1,0:T(1,128)} %get-tuple-element.580) | copy-start | bytes 3076
  27.8 6.5 %copy-start.70 = (f32[1,1,256]{2,1,0:T(1,128)S(1)}, f32[1,1,256]{2,1,0:T(1,128)}, u32[]{:S(2)}) copy-start(f32[1,1,256]{2,1,0:T(1,128)} %get-tuple-element.585) | copy-start | bytes 3076
  27.8 6.5 %copy-start.72 = (f32[1,1,256]{2,1,0:T(1,128)S(1)}, f32[1,1,256]{2,1,0:T(1,128)}, u32[]{:S(2)}) copy-start(f32[1,1,256]{2,1,0:T(1,128)} %get-tuple-element.586) | copy-start | bytes 3076
  27.9 6.5 %copy-start.74 = (f32[1,1,256]{2,1,0:T(1,128)S(1)}, f32[1,1,256]{2,1,0:T(1,128)}, u32[]{:S(2)}) copy-start(f32[1,1,256]{2,1,0:T(1,128)} %get-tuple-element.581) | copy-start | bytes 3076
  27.9 6.5 %copy-start.76 = (f32[1,1,256]{2,1,0:T(1,128)S(1)}, f32[1,1,256]{2,1,0:T(1,128)}, u32[]{:S(2)}) copy-start(f32[1,1,256]{2,1,0:T(1,128)} %get-tuple-element.582) | copy-start | bytes 3076
  27.9 6.5 %copy-start.78 = (f32[1,1,256]{2,1,0:T(1,128)S(1)}, f32[1,1,256]{2,1,0:T(1,128)}, u32[]{:S(2)}) copy-start(f32[1,1,256]{2,1,0:T(1,128)} %get-tuple-element.583) | copy-start | bytes 3076
  27.9 6.5 %copy-start.80 = (f32[1,1,256]{2,1,0:T(1,128)S(1)}, f32[1,1,256]{2,1,0:T(1,128)}, u32[]{:S(2)}) copy-start(f32[1,1,256]{2,1,0:T(1,128)} %get-tuple-element.584) | copy-start | bytes 3076
  27.9 8.2 %copy-start.44 = (f32[256,2,16]{0,2,1:T(8,128)S(1)}, f32[256,2,16]{0,2,1:T(8,128)}, u32[]{:S(2)}) copy-start(f32[256,2,16]{0,2,1:T(8,128)} %copy.231) | copy-start | bytes 98308
  34.3 86.7 %copy-start.3 = (bf16[256,2048]{0,1:T(8,128)(2,1)}, bf16[256,2048]{0,1:T(8,128)(2,1)S(1)}, u32[]{:S(2)}) copy-start(bf16[256,2048]{0,1:T(8,128)(2,1)S(1)} %get-tuple-element.538) | copy-start | bytes 3145732
  36.1 27.5 %copy-start.24 = (bf16[256,256]{0,1:T(8,128)(2,1)}, bf16[256,256]{0,1:T(8,128)(2,1)S(1)}, u32[]{:S(2)}) copy-start(bf16[256,256]{0,1:T(8,128)(2,1)S(1)} %get-tuple-element.540) | copy-start | bytes 393220
  36.1 20.3 %copy-start.32 = (f32[256,2,16]{2,1,0:T(2,128)S(1)}, f32[256,2,16]{2,1,0:T(2,128)}, u32[]{:S(2)}) copy-start(f32[256,2,16]{2,1,0:T(2,128)} %get-tuple-element.536) | copy-start | bytes 98308
  36.1 21.0 %copy-start.101 = (f32[32]{0:T(128)S(1)}, f32[32]{0:T(128)}, u32[]{:S(2)}) copy-start(f32[32]{0:T(128)} %get-tuple-element.493) | copy-start | bytes 388
  37.4 57.4 %all-gather.14.cloned.1.call-start = ((), (), s32[]{:S(2)}) async-start(), calls=%async_computation | async-start | bytes 1310720 | tf_op jit(solution)/shard_map/all_gather | solution.py:34
  63.6 108.5 %all-gather.18.cloned.1.call-start = ((), (), s32[]{:S(2)}) async-start(), calls=%async_computation.2 | async-start | bytes 2621440 | tf_op jit(solution)/shard_map/all_gather | solution.py:57
  99.9 3.5 %copy-start.15 = (f32[2,16,64,256]{3,2,1,0:T(8,128)}, f32[2,16,64,256]{3,2,1,0:T(8,128)S(1)}, u32[]{:S(2)}) copy-start(f32[2,16,64,256]{3,2,1,0:T(8,128)S(1)} %fusion.95) | copy-start | bytes 6291460
  103.4 12.3 %copy-start = (f32[1,256,2,16,64]{1,4,3,2,0:T(8,128)}, f32[1,256,2,16,64]{1,4,3,2,0:T(8,128)S(1)}, u32[]{:S(2)}) copy-start(f32[1,256,2,16,64]{1,4,3,2,0:T(8,128)S(1)} %fusion.32) | copy-start | bytes 6291460
  112.1 3.6 %copy-start.82 = (f32[256]{0:T(256)}, f32[256]{0:T(256)S(1)}, u32[]{:S(2)}) copy-start(f32[256]{0:T(256)S(1)} %add_rsqrt_fusion) | copy-start | bytes 3076
  121.0 4.9 %copy-start.43 = (f32[256,2,16]{0,2,1:T(8,128)S(1)}, f32[256,2,16]{0,2,1:T(8,128)}, u32[]{:S(2)}) copy-start(f32[256,2,16]{0,2,1:T(8,128)} %copy.234) | copy-start | bytes 98308
  121.0 4.9 %copy-start.86 = (f32[2,16]{1,0:T(2,128)S(1)}, f32[2,16]{1,0:T(2,128)}, u32[]{:S(2)}) copy-start(f32[2,16]{1,0:T(2,128)} %exponential_multiply_fusion) | copy-start | bytes 388
  161.3 3.5 %copy-start.25 = (bf16[256,256]{0,1:T(8,128)(2,1)S(1)}, bf16[256,256]{0,1:T(8,128)(2,1)}, u32[]{:S(2)}) copy-start(bf16[256,256]{0,1:T(8,128)(2,1)} %copy-done.24) | copy-start | bytes 393220
  161.3 3.5 %copy-start.33 = (bf16[2,256,256]{2,1,0:T(8,128)(2,1)S(1)}, bf16[2,256,256]{2,1,0:T(8,128)(2,1)}, u32[]{:S(2)}) copy-start(bf16[2,256,256]{2,1,0:T(8,128)(2,1)} %get-tuple-element.475) | copy-start | bytes 786436
  188.8 3.3 %copy-start.2 = (f32[256,2048]{0,1:T(8,128)S(1)}, f32[256,2048]{0,1:T(8,128)}, u32[]{:S(2)}) copy-start(f32[256,2048]{0,1:T(8,128)} %copy-done.1) | copy-start | bytes 6291460
  192.1 4.7 %copy-start.51 = (f32[1,2048]{1,0:T(1,128)S(1)}, f32[1,2048]{1,0:T(1,128)}, u32[]{:S(2)}) copy-start(f32[1,2048]{1,0:T(1,128)} %copy-done.50) | copy-start | bytes 24580
  192.1 4.7 %copy-start.53 = (f32[1,2048]{1,0:T(1,128)S(1)}, f32[1,2048]{1,0:T(1,128)}, u32[]{:S(2)}) copy-start(f32[1,2048]{1,0:T(1,128)} %copy-done.52) | copy-start | bytes 24580
  201.2 4.2 %copy-start.87 = (f32[2,16]{1,0:T(2,128)S(1)}, f32[2,16]{1,0:T(2,128)}, u32[]{:S(2)}) copy-start(f32[2,16]{1,0:T(2,128)} %multiply_reduce_fusion.6) | copy-start | bytes 388
  203.1 9.5 %copy-start.97 = (f32[2,16]{1,0:T(2,128)S(1)}, f32[2,16]{1,0:T(2,128)}, u32[]{:S(2)}) copy-start(f32[2,16]{1,0:T(2,128)} %copy-done.96) | copy-start | bytes 388
  203.1 9.5 %copy-start.13 = (f32[1,256,2,16]{3,2,1,0:T(2,128)S(1)}, f32[1,256,2,16]{3,2,1,0:T(2,128)}, u32[]{:S(2)}) copy-start(f32[1,256,2,16]{3,2,1,0:T(2,128)} %copy-done.12) | copy-start | bytes 98308
  203.1 9.5 %copy-start.34 = (f32[2,16,256]{1,0,2:T(2,128)S(1)}, f32[2,16,256]{1,0,2:T(2,128)}, u32[]{:S(2)}) copy-start(f32[2,16,256]{1,0,2:T(2,128)} %copy.244) | copy-start | bytes 98308
  205.4 7.8 %copy-start.46 = (f32[256,32]{0,1:T(8,128)S(1)}, f32[256,32]{0,1:T(8,128)}, u32[]{:S(2)}) copy-start(f32[256,32]{0,1:T(8,128)} %param.24) | copy-start | bytes 98308
  205.4 7.8 %copy-start.85 = (f32[32]{0:T(128)S(1)}, f32[32]{0:T(128)}, u32[]{:S(2)}) copy-start(f32[32]{0:T(128)} %copy-done.84) | copy-start | bytes 388
  205.4 10.6 %slice-start = ((f32[259,2048]{0,1:T(8,128)}), f32[3,2048]{0,1:T(8,128)S(1)}, s32[]{:S(2)}) async-start(f32[259,2048]{0,1:T(8,128)} %copy-done.7), calls=%async_computation.3 | async-start | bytes 2097152 | tf_op jit(solution)/shard_map/transpose(jvp())/split | solution.py:146
  205.4 10.6 %copy-start.38 = (f32[3,256]{0,1:T(8,128)S(1)}, f32[3,256]{0,1:T(8,128)}, u32[]{:S(2)}) copy-start(f32[3,256]{0,1:T(8,128)} %pad_add_fusion.9) | copy-start | bytes 9220
  213.2 4.7 %copy-start.92 = (f32[256]{0:T(256)S(1)}, f32[256]{0:T(256)}, u32[]{:S(2)}) copy-start(f32[256]{0:T(256)} %get-tuple-element.485) | copy-start | bytes 3076
  213.2 4.7 %copy-start.93 = (f32[256]{0:T(256)S(1)}, f32[256]{0:T(256)}, u32[]{:S(2)}) copy-start(f32[256]{0:T(256)} %get-tuple-element.490) | copy-start | bytes 3076
  213.2 4.7 %copy-start.94 = (f32[256]{0:T(256)S(1)}, f32[256]{0:T(256)}, u32[]{:S(2)}) copy-start(f32[256]{0:T(256)} %get-tuple-element.491) | copy-start | bytes 3076
  213.2 4.7 %copy-start.95 = (f32[256]{0:T(256)S(1)}, f32[256]{0:T(256)}, u32[]{:S(2)}) copy-start(f32[256]{0:T(256)} %get-tuple-element.492) | copy-start | bytes 3076
  213.2 4.7 %copy-start.88 = (f32[256]{0:T(256)S(1)}, f32[256]{0:T(256)}, u32[]{:S(2)}) copy-start(f32[256]{0:T(256)} %get-tuple-element.486) | copy-start | bytes 3076
  213.2 4.7 %copy-start.89 = (f32[256]{0:T(256)S(1)}, f32[256]{0:T(256)}, u32[]{:S(2)}) copy-start(f32[256]{0:T(256)} %get-tuple-element.487) | copy-start | bytes 3076
  213.2 4.7 %copy-start.90 = (f32[256]{0:T(256)S(1)}, f32[256]{0:T(256)}, u32[]{:S(2)}) copy-start(f32[256]{0:T(256)} %get-tuple-element.488) | copy-start | bytes 3076
  213.2 4.7 %copy-start.91 = (f32[256]{0:T(256)S(1)}, f32[256]{0:T(256)}, u32[]{:S(2)}) copy-start(f32[256]{0:T(256)} %get-tuple-element.489) | copy-start | bytes 3076
  213.2 5.3 %copy-start.18 = (f32[1,256,256]{1,2,0:T(8,128)S(1)}, f32[1,256,256]{1,2,0:T(8,128)}, u32[]{:S(2)}) copy-start(f32[1,256,256]{1,2,0:T(8,128)} %fusion.88) | copy-start | bytes 786436
  213.3 5.3 %copy-start.19 = (f32[1,256,256]{1,2,0:T(8,128)S(1)}, f32[1,256,256]{1,2,0:T(8,128)}, u32[]{:S(2)}) copy-start(f32[1,256,256]{1,2,0:T(8,128)} %fusion.87) | copy-start | bytes 786436
  216.0 3.9 %copy-start.58 = (f32[2048]{0:T(1024)S(1)}, f32[2048]{0:T(1024)}, u32[]{:S(2)}) copy-start(f32[2048]{0:T(1024)} %get-tuple-element.469) | copy-start | bytes 24580
  216.0 4.9 %copy-start.57 = (f32[2048]{0:T(1024)S(1)}, f32[2048]{0:T(1024)}, u32[]{:S(2)}) copy-start(f32[2048]{0:T(1024)} %get-tuple-element.476) | copy-start | bytes 24580
  216.1 3.8 %copy-start.59 = (f32[2048]{0:T(1024)S(1)}, f32[2048]{0:T(1024)}, u32[]{:S(2)}) copy-start(f32[2048]{0:T(1024)} %get-tuple-element.470) | copy-start | bytes 24580
  216.1 3.8 %copy-start.60 = (f32[2048]{0:T(1024)S(1)}, f32[2048]{0:T(1024)}, u32[]{:S(2)}) copy-start(f32[2048]{0:T(1024)} %get-tuple-element.471) | copy-start | bytes 24580
  216.5 25.2 %collective-permute-start.1 = (f32[3,2560]{1,0:T(4,128)S(1)}, f32[3,2560]{1,0:T(4,128)S(1)}, u32[]{:S(2)}, u32[]{:S(2)}) collective-permute-start(f32[3,2560]{1,0:T(4,128)S(1)} %copy.239), channel_id=1, source_target_pairs={{4,0},{8,4},{12,8},{5,1},{9,5},{13,9},{6,2},{10,6},{14,10},{7,3},{... | collective-permute-start | bytes 92168 | tf_op jit(solution)/shard_map/ppermute | solution.py:28
  219.3 33.1 %copy-start.8 = (f32[259,2048]{0,1:T(8,128)S(1)}, f32[259,2048]{0,1:T(8,128)}, u32[]{:S(2)}) copy-start(f32[259,2048]{0,1:T(8,128)} %copy-done.7) | copy-start | bytes 6365188
  (46 other events, 82.9 us)
Sparse Core Ops, SparseCore 0:
  37.6 28.2 all-gather.15
  67.4 27.3 all-gather.13
  127.2 44.8 all-gather.17
